TPU v7x, 32 devices: a whole 2x2x4 slice. The times are simulated.
32 devices in a mesh: grp: 4 (over y, x), inner: 8 (over z, core).
Axes of the slice: x: 2, y: 2, z: 4, core: 2. Of those that a mesh axis runs over, the one named last changes fastest.
Arguments:
- tokens: bfloat16 [512, 8192], P('inner', 'grp'), may hold values from -170 to 170
- norm_gain: bfloat16 [8192], P('grp'), may hold values from 0.5 to 2
- gate_up_weight: bfloat16 [2, 8192, 28672], P(None, 'grp', 'inner'), may hold values from -0.0625 to 0.0625
- down_weight: bfloat16 [28672, 8192], P('inner', 'grp'), may hold values from -0.03125 to 0.03125
- student_in: bfloat16 [512, 1024], P('grp'), may hold values from -6 to 6
- student_proj: bfloat16 [1024, 8192], P(None, 'inner'), may hold values from -0.1875 to 0.1875
Outputs:
- teacher_out: bfloat16 [512, 8192], P('inner', 'grp')
- grad_student: float32 [512, 1024], P('grp')
- grad_proj: float32 [1024, 8192], P(None, 'inner')
All inputs are finite; a program needn't handle non-finite values.
Results may differ from a plain program's by a relative error of at most 0.025.
Values may be sent and summed in bfloat16 or wider, within the bound.
No kernel may reach another device: no remote copies, remote signals or barrier semaphores. Data moves between devices by JAX's collectives and lax.ppermute only.
A program may use at most 128 MiB of HBM per device.

v0:
```python
import jax
import jax.numpy as jnp
from jax import lax
from jax.sharding import PartitionSpec as P

D = 8192


def activate(gate_up):
    return (jax.nn.silu(gate_up[:, 0, :]) * gate_up[:, 1, :]).astype(jnp.bfloat16)


def shards(tokens, norm_gain, gate_up_weight, down_weight, student_in, student_proj):
    values = tokens.astype(jnp.float32)
    squares = jnp.sum(values * values, axis=1)
    row_total = lax.psum(squares, "grp")
    inverse = lax.rsqrt(row_total / D + 1e-05)
    normed = (values * inverse[:, None] * norm_gain.astype(jnp.float32)[None, :]).astype(
        jnp.bfloat16
    )
    gathered = lax.all_gather(normed, "inner", axis=0, tiled=True)
    row_block = gathered
    shares = lax.psum_scatter(
        jnp.einsum(
            "rd,kdf->rkf", row_block, gate_up_weight, preferred_element_type=jnp.float32
        ).astype(jnp.bfloat16),
        "grp",
        scatter_dimension=0,
        tiled=True,
    ).astype(jnp.float32)
    hidden = lax.all_gather(activate(shares), "grp", axis=0, tiled=True)
    row_block = hidden
    teacher_out = lax.psum_scatter(
        jnp.dot(row_block, down_weight, preferred_element_type=jnp.float32).astype(jnp.bfloat16),
        "inner",
        scatter_dimension=0,
        tiled=True,
    )
    own_rows = student_in.shape[0]
    inner_count = lax.axis_size("inner")
    local_rows = teacher_out.shape[0]
    local_cols = teacher_out.shape[1]
    split_cols = teacher_out.reshape(local_rows, local_cols // inner_count, inner_count)
    first_move = lax.all_to_all(split_cols, "inner", split_axis=2, concat_axis=0, tiled=True)
    first_move = first_move.reshape(local_rows * inner_count, local_cols // inner_count)
    second_move = lax.all_to_all(first_move, "grp", split_axis=0, concat_axis=1, tiled=True)
    target_cols = second_move.shape[1]
    third_move = lax.all_to_all(
        second_move.reshape(own_rows, target_cols, 1),
        "inner",
        split_axis=1,
        concat_axis=2,
        tiled=True,
    )
    target = third_move.reshape(own_rows, target_cols)
    predicted = jnp.tanh(jnp.dot(student_in, student_proj, preferred_element_type=jnp.float32))
    mismatch = predicted - target.astype(jnp.float32)
    pre_grad = (mismatch * (1.0 - predicted * predicted)).astype(jnp.bfloat16)
    input_term = lax.dot_general(
        pre_grad, student_proj, (((1,), (1,)), ((), ())), preferred_element_type=jnp.float32
    )
    grad_student = lax.psum(input_term.astype(jnp.bfloat16), "inner").astype(jnp.float32)
    weight_term = lax.dot_general(
        student_in, pre_grad, (((0,), (0,)), ((), ())), preferred_element_type=jnp.float32
    )
    grad_proj = lax.psum(weight_term.astype(jnp.bfloat16), "grp").astype(jnp.float32)
    return (teacher_out, grad_student, grad_proj)


def solution(mesh):
    return jax.shard_map(
        shards,
        mesh=mesh,
        in_specs=(
            P("inner", "grp"),
            P("grp"),
            P(None, "grp", "inner"),
            P("inner", "grp"),
            P("grp", None),
            P(None, "inner"),
        ),
        out_specs=(P("inner", "grp"), P("grp", None), P(None, "inner")),
        check_vma=False,
    )
```

profile of v0, /device:TPU:0, one launch (start us, length us, event | category | flops | bytes accessed | tf_op | source)
XLA Modules:
  0.0 431.0 jit_solution(6755149970281105118)
XLA Ops:
  7.2 0.0 copy-start
  7.2 0.0 all-gather.3.cloned.1.call-start
  7.2 0.8 convert_element_type.52
  8.1 1.1 fusion.3
  9.2 11.4 %psum.21 = f32[64]{0:T(128)S(1)} all-reduce(f32[64]{0:T(128)S(1)} %fusion.3), channel_id=1, replica_groups=mesh['grp'=4,'inner'=8] {'grp'}, use_global_device_ids=true, to_apply=%region_1.0 | all-reduce | flops 64 | bytes 512 | tf_op jit(solution)/shard_map/psum | solution.py:16
  20.6 1.8 fusion.5
  22.3 0.0 all-gather.3.cloned.1.call-update
  22.4 0.0 reduce-scatter.3.cloned.1.call-start
  22.4 28.6 %all-gather.3.cloned.1.call-done = bf16[512,2048]{1,0:T(8,128)(2,1)} async-done(((bf16[64,2048]{1,0:T(8,128)(2,1)}), bf16[512,2048]{1,0:T(8,128)(2,1)}) %all-gather.3.cloned.1.call-update) | async-done | bytes 2097168 | tf_op jit(solution)/shard_map/all_gather | solution.py:21
  51.0 23.2 %convolution_convert_fusion = bf16[512,2,3584]{2,0,1:T(8,128)(2,1)} fusion(bf16[2,2048,3584]{2,1,0:T(8,128)(2,1)} %param.8, bf16[512,2048]{1,0:T(8,128)(2,1)} %all-gather.3.cloned.1.call-done), kind=kOutput, calls=%fused_computation | convolution fusion | flops 15036055552 | bytes 38797312 | tf_op jit(solution)/shard_map/rd,kdf->rkf/dot_general | solution.py:24
  74.2 0.0 reduce-scatter.3.cloned.1.call-update
  74.2 0.0 all-gather.5.cloned.1.call-start
  74.3 78.2 %reduce-scatter.3.cloned.1.call-done = bf16[128,2,3584]{2,0,1:T(8,128)(2,1)} async-done(((bf16[512,2,3584]{2,0,1:T(8,128)(2,1)}), bf16[128,2,3584]{2,0,1:T(8,128)(2,1)}) %reduce-scatter.3.cloned.1.call-update) | async-done | bytes 1835024 | tf_op jit(solution)/shard_map/reduce_scatter | solution.py:23
  152.5 1.9 convert_element_type.55
  154.4 1.4 fusion.2
  155.9 0.0 all-gather.5.cloned.1.call-update
  155.9 0.0 reduce-scatter.5.cloned.1.call-start
  156.0 48.3 %all-gather.5.cloned.1.call-done = bf16[512,3584]{1,0:T(8,128)(2,1)} async-done(((bf16[128,3584]{1,0:T(8,128)(2,1)}), bf16[512,3584]{1,0:T(8,128)(2,1)}) %all-gather.5.cloned.1.call-update) | async-done | bytes 3670032 | tf_op jit(solution)/shard_map/all_gather | solution.py:31
  204.3 13.0 %convolution_convert_fusion.1 = bf16[512,2048]{1,0:T(8,128)(2,1)} fusion(bf16[512,3584]{1,0:T(8,128)(2,1)} %all-gather.5.cloned.1.call-done, bf16[3584,2048]{1,0:T(8,128)(2,1)} %param.9), kind=kOutput, calls=%fused_computation.1 | convolution fusion | flops 7517241344 | bytes 20447232 | tf_op jit(solution)/shard_map/dot_general | solution.py:34
  217.3 0.0 reduce-scatter.5.cloned.1.call-update
  217.3 0.0 all-reduce.3.cloned.1.call-start
  217.4 36.2 %reduce-scatter.5.cloned.1.call-done = bf16[64,2048]{1,0:T(8,128)(2,1)} async-done(((bf16[512,2048]{1,0:T(8,128)(2,1)}), bf16[64,2048]{1,0:T(8,128)(2,1)}) %reduce-scatter.5.cloned.1.call-update) | async-done | bytes 262160 | tf_op jit(solution)/shard_map/reduce_scatter | solution.py:33
  253.5 1.2 copy.16
  254.8 0.3 copy.17
  255.1 12.1 %all_to_all.40 = bf16[64,256,8]{1,0,2:T(8,128)(2,1)S(1)} all-to-all(bf16[64,256,8]{1,0,2:T(8,128)(2,1)S(1)} %copy.17), channel_id=1, replica_groups=mesh['grp'=4,'inner'=8] {'inner'}, dimensions={2} | all-to-all | bytes 524288 | tf_op jit(solution)/shard_map/all_to_all | solution.py:44
  267.2 9.1 %all_to_all.41 = bf16[4,128,256]{2,1,0:T(8,128)(2,1)S(1)} all-to-all(bf16[4,128,256]{2,1,0:T(8,128)(2,1)S(1)} %bitcast.49), channel_id=1, replica_groups=mesh['grp'=4,'inner'=8] {'grp'}, dimensions={0} | all-to-all | bytes 524288 | tf_op jit(solution)/shard_map/all_to_all | solution.py:46
  276.3 0.2 copy.18
  276.5 0.4 copy.27
  276.9 0.5 broadcast.5
  277.4 2.2 reduce
  279.7 0.1 reshape.32
  279.7 12.3 %all_to_all.42 = bf16[8,2,8192]{2,1,0:T(2,128)(2,1)S(1)} all-to-all(bf16[8,2,8192]{2,1,0:T(2,128)(2,1)S(1)} %reshape.32), channel_id=1, replica_groups=mesh['grp'=4,'inner'=8] {'inner'}, dimensions={0} | all-to-all | bytes 524288 | tf_op jit(solution)/shard_map/all_to_all | solution.py:48
  292.0 0.0 copy-start.1
  292.0 0.3 reshape.33
  292.4 0.3 copy.26
  292.7 0.2 copy.22
  292.9 0.0 copy-done
  292.9 0.1 copy-done.1
  293.0 0.5 multiply_convert_fusion
  293.4 1.5 convolution_convert_fusion.2
  295.0 0.0 all-reduce.3.cloned.1.call-update
  295.0 0.0 all-reduce.5.cloned.1.call-start
  295.0 2.1 convert_bitcast_fusion
  297.1 0.0 all-reduce.5.cloned.1.call-update
  297.1 50.9 %all-reduce.3.cloned.1.call-done = bf16[128,1024]{1,0:T(8,128)(2,1)} async-done(((bf16[128,1024]{1,0:T(8,128)(2,1)}), bf16[128,1024]{1,0:T(8,128)(2,1)}) %all-reduce.3.cloned.1.call-update) | async-done | bytes 262160 | tf_op jit(solution)/shard_map/psum | solution.py:62
  348.0 1.8 convert_element_type.64
  349.8 70.3 %all-reduce.5.cloned.1.call-done = bf16[1024,1024]{0,1:T(8,128)(2,1)} async-done(((bf16[1024,1024]{0,1:T(8,128)(2,1)}), bf16[1024,1024]{0,1:T(8,128)(2,1)}) %all-reduce.5.cloned.1.call-update) | async-done | bytes 2097168 | tf_op jit(solution)/shard_map/psum | solution.py:66
  420.1 4.1 copy.23
  (3 shorter events, 0.1 us)
Async XLA Ops:
  7.2 285.7 %copy-start = (bf16[1024,1024]{1,0:T(8,128)(2,1)S(1)}, bf16[1024,1024]{1,0:T(8,128)(2,1)}, u32[]{:S(2)}) copy-start(bf16[1024,1024]{1,0:T(8,128)(2,1)} %param.11) | copy-start | bytes 6291460
  7.2 43.9 %all-gather.3.cloned.1.call-start = ((), (), s32[]{:S(2)}) async-start(), calls=%async_computation.5 | async-start | bytes 2359296 | tf_op jit(solution)/shard_map/all_gather | solution.py:21
  22.4 130.2 %reduce-scatter.3.cloned.1.call-start = ((), (), s32[]{:S(2)}) async-start(), calls=%async_computation.6 | async-start | bytes 9175040 | tf_op jit(solution)/shard_map/reduce_scatter | solution.py:23
  74.2 130.0 %all-gather.5.cloned.1.call-start = ((), (), s32[]{:S(2)}) async-start(), calls=%async_computation.7 | async-start | bytes 4587520 | tf_op jit(solution)/shard_map/all_gather | solution.py:31
  155.9 97.6 %reduce-scatter.5.cloned.1.call-start = ((), (), s32[]{:S(2)}) async-start(), calls=%async_computation.8 | async-start | bytes 2359296 | tf_op jit(solution)/shard_map/reduce_scatter | solution.py:33
  217.3 130.7 %all-reduce.3.cloned.1.call-start = ((), (), s32[]{:S(2)}) async-start(), calls=%async_computation.9 | async-start | bytes 524288 | tf_op jit(solution)/shard_map/psum | solution.py:62
  292.0 1.0 copy-start.1
  295.0 125.1 %all-reduce.5.cloned.1.call-start = ((), (), s32[]{:S(2)}) async-start(), calls=%async_computation.10 | async-start | bytes 4194304 | tf_op jit(solution)/shard_map/psum | solution.py:66
Sparse Core Ops, SparseCore 0:
  22.5 28.5 all-gather.2
  74.3 78.1 reduce-scatter.2
  156.0 48.1 all-gather.4
  217.4 36.0 reduce-scatter.4
  295.1 52.8 all-reduce.2
  351.5 68.5 all-reduce.4
where the time goes:
time: 432 us; the launch traced here: 431 us
  waiting for transfers between devices  313 us (72%)
  blocking collectives  44.9 us (10%)
  matrix products  40.2 us (9%)
  between operations  14.2 us (3%)
  other arithmetic  11.1 us (3%)
  local copies, waits for them, and re-layouts  7.68 us (2%)
    reduce_scatter x1, waiting for transfers between devices, shards(): lax.psum_scatter(jnp.einsum('rd,kdf->rkf', row_block, gate_up_weight, pre...  78.2 us
    psum x1, waiting for transfers between devices, shards(): lax.psum(weight_term.astype(jnp.bfloat16), 'grp').astype(jnp.float32)  70.3 us
    psum x1, waiting for transfers between devices, shards(): lax.psum(input_term.astype(jnp.bfloat16), 'inner').astype(jnp.float32)  50.9 us
    all_gather x1, waiting for transfers between devices, shards(): hidden = lax.all_gather(activate(shares), 'grp', axis=0, tiled=True)  48.3 us
    reduce_scatter x1, waiting for transfers between devices, shards(): lax.psum_scatter(jnp.dot(row_block, down_weight, preferred_element_type=j...  36.2 us
    all_gather x1, waiting for transfers between devices, shards(): gathered = lax.all_gather(normed, 'inner', axis=0, tiled=True)  28.6 us
    dot_general x1, matrix products, shards(): jnp.einsum('rd,kdf->rkf', row_block, gate_up_weight, preferred_element_ty...  23.2 us
    dot_general x1, matrix products, shards(): jnp.dot(row_block, down_weight, preferred_element_type=jnp.float32)  13 us
  transfers between devices with their start and end apart: 6, of which 6 were waited for; matrix products, arithmetic and copies ran while one was open for 1% of the time, Pallas kernels for 0%

commit v1 on v0

--- a/solution.py
+++ b/solution.py
@@ -63,7 +63,9 @@
     weight_term = lax.dot_general(
         student_in, pre_grad, (((0,), (0,)), ((), ())), preferred_element_type=jnp.float32
     )
-    grad_proj = lax.psum(weight_term.astype(jnp.bfloat16), "grp").astype(jnp.float32)
+    grad_proj = jnp.sum(lax.all_gather(weight_term.astype(jnp.bfloat16), "grp"), axis=0).astype(
+        jnp.float32
+    )
     return (teacher_out, grad_student, grad_proj)
 
 

time: 432 us -> 476 us (1.10)
  waiting for transfers between devices: 313 us -> 329 us
  local copies, waits for them, and re-layouts: 7.68 us -> 22.2 us
  other arithmetic: 11.1 us -> 24 us
    all_gather x0 -> x1, waiting for transfers between devices: none -> 87 us  [shards(): lax.all_gather(weight_term.astype(jnp.bfloat16), 'grp')]
    psum x1 -> x0, waiting for transfers between devices: 70.3 us -> none  [shards(): lax.psum(weight_term.astype(jnp.bfloat16), 'grp').astype(jnp.float32)]
    all_gather x0 -> x1, local copies, waits for them, and re-layouts: none -> 14.6 us  [shards(): lax.all_gather(weight_term.astype(jnp.bfloat16), 'grp')]
    reduce_sum x0 -> x1, other arithmetic: none -> 12.9 us  [shards(): jnp.sum(lax.all_gather(weight_term.astype(jnp.bfloat16), 'grp'), axis=0)]
where the time goes in v1:
time: 476 us; the launch traced here: 475 us
  waiting for transfers between devices  329 us (69%)
  blocking collectives  44.9 us (9%)
  matrix products  40.2 us (8%)
  other arithmetic  24 us (5%)
  local copies, waits for them, and re-layouts  22.2 us (5%)
  between operations  14.2 us (3%)
    all_gather x1, waiting for transfers between devices, shards(): lax.all_gather(weight_term.astype(jnp.bfloat16), 'grp')  87 us
    reduce_scatter x1, waiting for transfers between devices, shards(): lax.psum_scatter(jnp.einsum('rd,kdf->rkf', row_block, gate_up_weight, pre...  78.2 us
    psum x1, waiting for transfers between devices, shards(): lax.psum(input_term.astype(jnp.bfloat16), 'inner').astype(jnp.float32)  50.9 us
    all_gather x1, waiting for transfers between devices, shards(): hidden = lax.all_gather(activate(shares), 'grp', axis=0, tiled=True)  48.3 us
    reduce_scatter x1, waiting for transfers between devices, shards(): lax.psum_scatter(jnp.dot(row_block, down_weight, preferred_element_type=j...  36.2 us
    all_gather x1, waiting for transfers between devices, shards(): gathered = lax.all_gather(normed, 'inner', axis=0, tiled=True)  28.6 us
    dot_general x1, matrix products, shards(): jnp.einsum('rd,kdf->rkf', row_block, gate_up_weight, preferred_element_ty...  23.2 us
    all_gather x1, local copies, waits for them, and re-layouts, shards(): lax.all_gather(weight_term.astype(jnp.bfloat16), 'grp')  14.6 us
  transfers between devices with their start and end apart: 6, of which 6 were waited for; matrix products, arithmetic and copies ran while one was open for 1% of the time, Pallas kernels for 0%

profile of v1, /device:TPU:0, one launch (start us, length us, event | category | flops | bytes accessed | tf_op | source)
XLA Modules:
  0.0 475.2 jit_solution(15153864293041737538)
XLA Ops:
  7.2 0.0 copy-start
  7.2 0.0 all-gather.5.cloned.1.call-start
  7.2 0.8 convert_element_type.54
  8.1 1.1 fusion.3
  9.2 11.4 %psum.14 = f32[64]{0:T(128)S(1)} all-reduce(f32[64]{0:T(128)S(1)} %fusion.3), channel_id=1, replica_groups=mesh['grp'=4,'inner'=8] {'grp'}, use_global_device_ids=true, to_apply=%region_1.0 | all-reduce | flops 64 | bytes 512 | tf_op jit(solution)/shard_map/psum | solution.py:16
  20.6 1.8 fusion.5
  22.3 0.0 all-gather.5.cloned.1.call-update
  22.4 0.0 reduce-scatter.3.cloned.1.call-start
  22.4 28.6 %all-gather.5.cloned.1.call-done = bf16[512,2048]{1,0:T(8,128)(2,1)} async-done(((bf16[64,2048]{1,0:T(8,128)(2,1)}), bf16[512,2048]{1,0:T(8,128)(2,1)}) %all-gather.5.cloned.1.call-update) | async-done | bytes 2097168 | tf_op jit(solution)/shard_map/all_gather | solution.py:21
  51.0 23.2 %convolution_convert_fusion = bf16[512,2,3584]{2,0,1:T(8,128)(2,1)} fusion(bf16[2,2048,3584]{2,1,0:T(8,128)(2,1)} %param.8, bf16[512,2048]{1,0:T(8,128)(2,1)} %all-gather.5.cloned.1.call-done), kind=kOutput, calls=%fused_computation | convolution fusion | flops 15036055552 | bytes 38797312 | tf_op jit(solution)/shard_map/rd,kdf->rkf/dot_general | solution.py:24
  74.2 0.0 reduce-scatter.3.cloned.1.call-update
  74.2 0.0 all-gather.7.cloned.1.call-start
  74.3 78.2 %reduce-scatter.3.cloned.1.call-done = bf16[128,2,3584]{2,0,1:T(8,128)(2,1)} async-done(((bf16[512,2,3584]{2,0,1:T(8,128)(2,1)}), bf16[128,2,3584]{2,0,1:T(8,128)(2,1)}) %reduce-scatter.3.cloned.1.call-update) | async-done | bytes 1835024 | tf_op jit(solution)/shard_map/reduce_scatter | solution.py:23
  152.5 1.9 convert_element_type.57
  154.4 1.4 fusion.2
  155.9 0.0 all-gather.7.cloned.1.call-update
  155.9 0.0 reduce-scatter.5.cloned.1.call-start
  156.0 48.3 %all-gather.7.cloned.1.call-done = bf16[512,3584]{1,0:T(8,128)(2,1)} async-done(((bf16[128,3584]{1,0:T(8,128)(2,1)}), bf16[512,3584]{1,0:T(8,128)(2,1)}) %all-gather.7.cloned.1.call-update) | async-done | bytes 3670032 | tf_op jit(solution)/shard_map/all_gather | solution.py:31
  204.3 13.0 %convolution_convert_fusion.1 = bf16[512,2048]{1,0:T(8,128)(2,1)} fusion(bf16[512,3584]{1,0:T(8,128)(2,1)} %all-gather.7.cloned.1.call-done, bf16[3584,2048]{1,0:T(8,128)(2,1)} %param.9), kind=kOutput, calls=%fused_computation.1 | convolution fusion | flops 7517241344 | bytes 20447232 | tf_op jit(solution)/shard_map/dot_general | solution.py:34
  217.3 0.0 reduce-scatter.5.cloned.1.call-update
  217.3 0.0 all-reduce.2.cloned.1.call-start
  217.4 36.2 %reduce-scatter.5.cloned.1.call-done = bf16[64,2048]{1,0:T(8,128)(2,1)} async-done(((bf16[512,2048]{1,0:T(8,128)(2,1)}), bf16[64,2048]{1,0:T(8,128)(2,1)}) %reduce-scatter.5.cloned.1.call-update) | async-done | bytes 262160 | tf_op jit(solution)/shard_map/reduce_scatter | solution.py:33
  253.5 1.2 copy.14
  254.8 0.3 copy.15
  255.1 12.1 %all_to_all.40 = bf16[64,256,8]{1,0,2:T(8,128)(2,1)S(1)} all-to-all(bf16[64,256,8]{1,0,2:T(8,128)(2,1)S(1)} %copy.15), channel_id=1, replica_groups=mesh['grp'=4,'inner'=8] {'inner'}, dimensions={2} | all-to-all | bytes 524288 | tf_op jit(solution)/shard_map/all_to_all | solution.py:44
  267.2 9.1 %all_to_all.41 = bf16[4,128,256]{2,1,0:T(8,128)(2,1)S(1)} all-to-all(bf16[4,128,256]{2,1,0:T(8,128)(2,1)S(1)} %bitcast.51), channel_id=1, replica_groups=mesh['grp'=4,'inner'=8] {'grp'}, dimensions={0} | all-to-all | bytes 524288 | tf_op jit(solution)/shard_map/all_to_all | solution.py:46
  276.3 0.2 copy.16
  276.5 0.4 copy.25
  276.9 0.5 broadcast.5
  277.4 2.2 reduce.1
  279.7 0.1 reshape.33
  279.7 12.3 %all_to_all.42 = bf16[8,2,8192]{2,1,0:T(2,128)(2,1)S(1)} all-to-all(bf16[8,2,8192]{2,1,0:T(2,128)(2,1)S(1)} %reshape.33), channel_id=1, replica_groups=mesh['grp'=4,'inner'=8] {'inner'}, dimensions={0} | all-to-all | bytes 524288 | tf_op jit(solution)/shard_map/all_to_all | solution.py:48
  292.0 0.3 reshape.34
  292.4 0.3 copy.24
  292.7 0.2 copy.20
  292.9 0.1 copy-done.1
  293.0 0.5 multiply_convert_fusion
  293.4 1.5 convolution_convert_fusion.2
  295.0 0.0 all-reduce.2.cloned.1.call-update
  295.0 0.0 all-gather.9.cloned.1.call-start
  295.0 2.1 convert_bitcast_fusion
  297.1 0.0 all-gather.9.cloned.1.call-update
  297.1 50.9 %all-reduce.2.cloned.1.call-done = bf16[128,1024]{1,0:T(8,128)(2,1)} async-done(((bf16[128,1024]{1,0:T(8,128)(2,1)}), bf16[128,1024]{1,0:T(8,128)(2,1)}) %all-reduce.2.cloned.1.call-update) | async-done | bytes 262160 | tf_op jit(solution)/shard_map/psum | solution.py:62
  348.0 1.8 convert_element_type.66
  349.8 87.0 %all-gather.9.cloned.1.call-done = bf16[4096,1024]{0,1:T(8,128)(2,1)} async-done(((bf16[1024,1024]{0,1:T(8,128)(2,1)}), bf16[4096,1024]{0,1:T(8,128)(2,1)}) %all-gather.9.cloned.1.call-update) | async-done | bytes 8388624 | tf_op jit(solution)/shard_map/all_gather | solution.py:66
  436.8 14.6 %reshape.31 = bf16[4,1024,1024]{1,0,2:T(4,128)(2,1)} reshape(bf16[4096,1024]{0,1:T(8,128)(2,1)} %all-gather.9.cloned.1.call-done) | data formatting | bytes 16777216 | tf_op jit(solution)/shard_map/all_gather | solution.py:66
  451.4 12.9 %reduce_sum.22 = bf16[1024,1024]{0,1:T(8,128)(2,1)} reduce(bf16[4,1024,1024]{1,0,2:T(4,128)(2,1)} %reshape.31, bf16[]{:T(256)} %constant.12.clone.1), dimensions={0}, to_apply=%region_5.6 | reduce | flops 3145728 | bytes 10485762 | tf_op jit(solution)/shard_map/reduce_sum | solution.py:66
  464.3 4.1 copy.21
  (5 shorter events, 0.1 us)
Async XLA Ops:
  7.2 285.7 %copy-start = (bf16[1024,1024]{1,0:T(8,128)(2,1)S(1)}, bf16[1024,1024]{1,0:T(8,128)(2,1)}, u32[]{:S(2)}) copy-start(bf16[1024,1024]{1,0:T(8,128)(2,1)} %param.11) | copy-start | bytes 6291460
  7.2 43.9 %all-gather.5.cloned.1.call-start = ((), (), s32[]{:S(2)}) async-start(), calls=%async_computation.5 | async-start | bytes 2359296 | tf_op jit(solution)/shard_map/all_gather | solution.py:21
  22.4 130.2 %reduce-scatter.3.cloned.1.call-start = ((), (), s32[]{:S(2)}) async-start(), calls=%async_computation.6 | async-start | bytes 9175040 | tf_op jit(solution)/shard_map/reduce_scatter | solution.py:23
  74.2 130.0 %all-gather.7.cloned.1.call-start = ((), (), s32[]{:S(2)}) async-start(), calls=%async_computation.7 | async-start | bytes 4587520 | tf_op jit(solution)/shard_map/all_gather | solution.py:31
  155.9 97.6 %reduce-scatter.5.cloned.1.call-start = ((), (), s32[]{:S(2)}) async-start(), calls=%async_computation.8 | async-start | bytes 2359296 | tf_op jit(solution)/shard_map/reduce_scatter | solution.py:33
  217.3 130.7 %all-reduce.2.cloned.1.call-start = ((), (), s32[]{:S(2)}) async-start(), calls=%async_computation.9 | async-start | bytes 524288 | tf_op jit(solution)/shard_map/psum | solution.py:62
  292.0 1.0 copy-start.1
  295.0 141.8 %all-gather.9.cloned.1.call-start = ((), (), s32[]{:S(2)}) async-start(), calls=%async_computation.10 | async-start | bytes 10485760 | tf_op jit(solution)/shard_map/all_gather | solution.py:66
Sparse Core Ops, SparseCore 0:
  22.5 28.5 all-gather.4
  74.3 78.1 reduce-scatter.2
  156.0 48.1 all-gather.6
  217.4 36.0 reduce-scatter.4
  295.1 52.8 all-reduce.1
  350.3 86.5 all-gather.8
